TPU v7x, 512 devices: a whole 4x4x16 slice. The times are simulated.
512 devices in a mesh: blk: 16 (over y_hi, x, core), wide: 32 (over y_lo, z).
Axes of the slice: x: 4, y: 4 (y_hi: 2, y_lo: 2; y = y_hi * 2 + y_lo), z: 16, core: 2. Of those that a mesh axis runs over, the one named last changes fastest.
Arguments:
- patch_keys: float32 [512, 196, 512], P(('blk', 'wide')), may hold values from -16 to 16
- patch_values: float32 [512, 196, 512], P(('blk', 'wide')), may hold values from -6 to 6
- caption_queries: float32 [512, 512], P(('blk', 'wide')), may hold values from -48 to 48
- positive: int32 [512, 512], P(('blk', 'wide')), may hold values 0 or 1
Outputs:
- grad_keys: float32 [512, 196, 512], P(('blk', 'wide'))
- grad_values: float32 [512, 196, 512], P(('blk', 'wide'))
- grad_queries: float32 [512, 512], P(('blk', 'wide'))
All inputs are finite; a program needn't handle non-finite values. No bound on the sum of `positive` on one device may be relied on, other than what follows from the above.
Results may differ from a plain program's by a relative error of at most 0.0005.
Values sent between devices are 32-bit elements; how exact they have to be, the bound alone decides.
No kernel may reach another device: no remote copies, remote signals or barrier semaphores. Data moves between devices by JAX's collectives and lax.ppermute only.
A program may use at most 64 MiB of HBM per device.

v0:
```python
import jax
import jax.numpy as jnp
from jax import lax
from jax.sharding import PartitionSpec as P

HEADS = 8
epsilon = 1e-06
similarity_multiplier = 10.0
similarity_shift_term = -2.0


def passed_along(value, axis, steps):
    count = lax.axis_size(axis)
    pairs = [(source, (source + steps) % count) for source in range(count)]
    return lax.ppermute(value, axis, pairs)


def pair_loss(keys, values, queries, labels):
    images, patches, width = keys.shape
    row_count = queries.shape[0]
    head_dim = width // HEADS
    query_heads = queries.reshape(row_count, HEADS, head_dim)
    key_heads = keys.reshape(images, patches, HEADS, head_dim)
    value_heads = values.reshape(images, patches, HEADS, head_dim)
    scores = jnp.einsum(
        "chd,iphd->ichp", query_heads, key_heads, precision=lax.Precision.HIGHEST
    ) * head_dim ** (-0.5)
    row_max = lax.stop_gradient(jnp.max(scores, axis=3, keepdims=True))
    exponent = jnp.exp(scores - row_max)
    weights = exponent / jnp.sum(exponent, axis=3, keepdims=True)
    pooled = jnp.einsum(
        "ichp,iphd->ichd", weights, value_heads, precision=lax.Precision.HIGHEST
    ).reshape(images, row_count, width)
    matching_similarity = jnp.mean(pooled * queries[None], axis=2)
    summary_reciprocal_length = lax.rsqrt(jnp.mean(pooled * pooled, axis=2) + epsilon)
    probe_reciprocal_length = lax.rsqrt(jnp.mean(queries * queries, axis=1) + epsilon)
    matching_scaled_scores = (
        similarity_multiplier
        * matching_similarity
        * summary_reciprocal_length
        * probe_reciprocal_length[None]
        + similarity_shift_term
    )
    label_signs = 2.0 * labels.astype(jnp.float32) - 1.0
    return jnp.sum(jnp.logaddexp(0.0, -label_signs * matching_scaled_scores))


def pair_grads(keys, values, queries, labels):

    def loss_of(keys_in, values_in, input_queries):
        return pair_loss(keys_in, values_in, input_queries, labels)

    total, pull_back = jax.vjp(loss_of, keys, values, queries)
    return pull_back(jnp.ones_like(total))


def per_device(patch_keys, patch_values, caption_queries, positive):
    caption_group = lax.all_gather(caption_queries, "wide", axis=0, tiled=True)
    group_rows = caption_group.shape[0]
    cycle_size = lax.axis_size("blk")
    cycle_home = lax.axis_index("blk")
    key_zero = jnp.zeros_like(patch_keys)
    value_zero = jnp.zeros_like(patch_values)

    def cycle_turn(turn, carried):
        key_grad, value_grad, evaluate_objective, forward_acc, backward, backward_acc = carried
        source = (cycle_home - turn) % cycle_size
        labels_fwd = lax.dynamic_slice_in_dim(positive, source * group_rows, group_rows, 1)
        visiting = evaluate_objective
        key_part, value_part, query_part = pair_grads(
            patch_keys, patch_values, visiting, labels_fwd
        )
        forward_acc = forward_acc + query_part
        backward_acc = backward_acc + query_part[group_rows:]
        evaluate_objective, forward_acc = passed_along((evaluate_objective, forward_acc), "blk", 1)
        return (
            key_grad + key_part,
            value_grad + value_part,
            evaluate_objective,
            forward_acc,
            backward,
            backward_acc,
        )

    backward_start = caption_group[group_rows:]
    initial = (
        key_zero,
        value_zero,
        caption_group,
        jnp.zeros_like(caption_group),
        backward_start,
        jnp.zeros_like(backward_start),
    )
    grad_keys, grad_values, forward_end, forward_acc, backward_end, backward_acc = lax.fori_loop(
        0, cycle_size, cycle_turn, initial
    )
    group_grad = jnp.concatenate([forward_acc, backward_acc], 0)
    grad_queries = lax.psum_scatter(group_grad, "wide", scatter_dimension=0, tiled=True)
    return (grad_keys, grad_values, grad_queries)


def solution(mesh):
    in_specs = (
        P(("blk", "wide"), None, None),
        P(("blk", "wide"), None, None),
        P(("blk", "wide"), None),
        P(("blk", "wide"), None),
    )
    out_specs = (
        P(("blk", "wide"), None, None),
        P(("blk", "wide"), None, None),
        P(("blk", "wide"), None),
    )
    return jax.shard_map(
        per_device, mesh=mesh, in_specs=in_specs, out_specs=out_specs, check_vma=False
    )
```

profile of v0, /device:TPU:2, one launch (start us, length us, event | category | flops | bytes accessed | tf_op | source)
XLA Modules:
  0.0 610.4 jit_solution(129645985034968549)
XLA Ops:
  9.2 69.2 %all-gather = f32[32,1,512]{2,1,0:T(1,128)S(1)} all-gather(f32[1,1,512]{2,1,0:T(1,128)S(1)} %bitcast.248), channel_id=1, replica_groups=mesh['blk'=16,'wide'=32] {'wide'}, dimensions={0}, use_global_device_ids=true | all-gather | bytes 67584 | tf_op jit(solution)/shard_map/all_gather | solution.py:58
  79.6 283.0 %while.23 = (s32[]{:T(128)}, f32[1,196,512]{1,2,0:T(8,128)S(1)}, f32[1,196,512]{1,2,0:T(8,128)S(1)}, f32[32,512]{1,0:T(8,128)}, f32[32,512]{1,0:T(8,128)}, /*ind...) while((s32[]{:T(128)}, f32[1,196,512]{1,2,0:T(8,128)S(1)}, ...), condition=%wide.region_7.8_spmd.clone, body=%wide.region_0.7_spmd.clone.sunk | while | flops 232979744 | bytes 9337618 | solution.py:94
  88.2 3.5 collective-permute-start.1
  96.3 1.9 collective-permute-start
  104.0 3.2 collective-permute-start.1
  119.5 4.8 collective-permute-start.1
  136.6 5.7 collective-permute-start.1
  147.0 1.9 collective-permute-start
  154.7 5.7 collective-permute-start.1
  165.0 1.9 collective-permute-start
  172.7 5.7 collective-permute-start.1
  190.8 5.7 collective-permute-start.1
  208.8 5.7 collective-permute-start.1
  219.2 1.9 collective-permute-start
  226.8 5.7 collective-permute-start.1
  244.9 5.7 collective-permute-start.1
  262.9 5.7 collective-permute-start.1
  281.0 5.7 collective-permute-start.1
  299.0 5.7 collective-permute-start.1
  309.4 1.9 collective-permute-start
  317.1 5.7 collective-permute-start.1
  335.1 5.7 collective-permute-start.1
  353.2 5.7 collective-permute-start.1
  366.0 235.7 %all-reduce.3.cloned.1.call-done = f32[32,512]{1,0:T(8,128)} async-done(((f32[32,512]{1,0:T(8,128)}), f32[32,512]{1,0:T(8,128)}) %all-reduce.3.cloned.1.call-update) | async-done | bytes 65552
  (411 shorter events, 193.1 us)
Async XLA Ops:
  7.2 594.5 %all-reduce.3.cloned.1.call-start = ((), (), s32[]{:S(2)}) async-start(), calls=%async_computation | async-start | bytes 131072
  80.5 14.9 %collective-permute-start = (f32[32,512]{1,0:T(8,128)S(1)}, f32[32,512]{1,0:T(8,128)}, u32[]{:S(2)}, u32[]{:S(2)}) collective-permute-start(f32[32,512]{1,0:T(8,128)S(1)} %copy.71), channel_id=1, source_target_pairs={{0,32},{32,64},{64,96},{96,128},{128,160},{160,192},{192,224},{224... | collective-permute-start | bytes 196616 | tf_op jit(solution)/shard_map/while/body/eval_jaxpr/ppermute | solution.py:15
  96.3 14.7 %collective-permute-start = (f32[32,512]{1,0:T(8,128)S(1)}, f32[32,512]{1,0:T(8,128)}, u32[]{:S(2)}, u32[]{:S(2)}) collective-permute-start(f32[32,512]{1,0:T(8,128)S(1)} %copy.71), channel_id=1, source_target_pairs={{0,32},{32,64},{64,96},{96,128},{128,160},{160,192},{192,224},{224... | collective-permute-start | bytes 196616 | tf_op jit(solution)/shard_map/while/body/eval_jaxpr/ppermute | solution.py:15
  111.8 16.3 %collective-permute-start = (f32[32,512]{1,0:T(8,128)S(1)}, f32[32,512]{1,0:T(8,128)}, u32[]{:S(2)}, u32[]{:S(2)}) collective-permute-start(f32[32,512]{1,0:T(8,128)S(1)} %copy.71), channel_id=1, source_target_pairs={{0,32},{32,64},{64,96},{96,128},{128,160},{160,192},{192,224},{224... | collective-permute-start | bytes 196616 | tf_op jit(solution)/shard_map/while/body/eval_jaxpr/ppermute | solution.py:15
  128.9 17.2 %collective-permute-start = (f32[32,512]{1,0:T(8,128)S(1)}, f32[32,512]{1,0:T(8,128)}, u32[]{:S(2)}, u32[]{:S(2)}) collective-permute-start(f32[32,512]{1,0:T(8,128)S(1)} %copy.71), channel_id=1, source_target_pairs={{0,32},{32,64},{64,96},{96,128},{128,160},{160,192},{192,224},{224... | collective-permute-start | bytes 196616 | tf_op jit(solution)/shard_map/while/body/eval_jaxpr/ppermute | solution.py:15
  147.0 17.2 %collective-permute-start = (f32[32,512]{1,0:T(8,128)S(1)}, f32[32,512]{1,0:T(8,128)}, u32[]{:S(2)}, u32[]{:S(2)}) collective-permute-start(f32[32,512]{1,0:T(8,128)S(1)} %copy.71), channel_id=1, source_target_pairs={{0,32},{32,64},{64,96},{96,128},{128,160},{160,192},{192,224},{224... | collective-permute-start | bytes 196616 | tf_op jit(solution)/shard_map/while/body/eval_jaxpr/ppermute | solution.py:15
  154.7 9.5 %collective-permute-start.1 = (f32[32,512]{1,0:T(8,128)}, f32[32,512]{1,0:T(8,128)}, u32[]{:S(2)}, u32[]{:S(2)}) collective-permute-start(f32[32,512]{1,0:T(8,128)} %fusion.71), channel_id=1, source_target_pairs={{0,32},{32,64},{64,96},{96,128},{128,160},{160,192},{192,224},{224... | collective-permute-start | bytes 196616 | tf_op jit(solution)/shard_map/while/body/eval_jaxpr/ppermute | solution.py:15
  165.0 17.2 %collective-permute-start = (f32[32,512]{1,0:T(8,128)S(1)}, f32[32,512]{1,0:T(8,128)}, u32[]{:S(2)}, u32[]{:S(2)}) collective-permute-start(f32[32,512]{1,0:T(8,128)S(1)} %copy.71), channel_id=1, source_target_pairs={{0,32},{32,64},{64,96},{96,128},{128,160},{160,192},{192,224},{224... | collective-permute-start | bytes 196616 | tf_op jit(solution)/shard_map/while/body/eval_jaxpr/ppermute | solution.py:15
  183.1 17.2 %collective-permute-start = (f32[32,512]{1,0:T(8,128)S(1)}, f32[32,512]{1,0:T(8,128)}, u32[]{:S(2)}, u32[]{:S(2)}) collective-permute-start(f32[32,512]{1,0:T(8,128)S(1)} %copy.71), channel_id=1, source_target_pairs={{0,32},{32,64},{64,96},{96,128},{128,160},{160,192},{192,224},{224... | collective-permute-start | bytes 196616 | tf_op jit(solution)/shard_map/while/body/eval_jaxpr/ppermute | solution.py:15
  190.8 9.5 %collective-permute-start.1 = (f32[32,512]{1,0:T(8,128)}, f32[32,512]{1,0:T(8,128)}, u32[]{:S(2)}, u32[]{:S(2)}) collective-permute-start(f32[32,512]{1,0:T(8,128)} %fusion.71), channel_id=1, source_target_pairs={{0,32},{32,64},{64,96},{96,128},{128,160},{160,192},{192,224},{224... | collective-permute-start | bytes 196616 | tf_op jit(solution)/shard_map/while/body/eval_jaxpr/ppermute | solution.py:15
  201.1 17.2 %collective-permute-start = (f32[32,512]{1,0:T(8,128)S(1)}, f32[32,512]{1,0:T(8,128)}, u32[]{:S(2)}, u32[]{:S(2)}) collective-permute-start(f32[32,512]{1,0:T(8,128)S(1)} %copy.71), channel_id=1, source_target_pairs={{0,32},{32,64},{64,96},{96,128},{128,160},{160,192},{192,224},{224... | collective-permute-start | bytes 196616 | tf_op jit(solution)/shard_map/while/body/eval_jaxpr/ppermute | solution.py:15
  219.2 17.2 %collective-permute-start = (f32[32,512]{1,0:T(8,128)S(1)}, f32[32,512]{1,0:T(8,128)}, u32[]{:S(2)}, u32[]{:S(2)}) collective-permute-start(f32[32,512]{1,0:T(8,128)S(1)} %copy.71), channel_id=1, source_target_pairs={{0,32},{32,64},{64,96},{96,128},{128,160},{160,192},{192,224},{224... | collective-permute-start | bytes 196616 | tf_op jit(solution)/shard_map/while/body/eval_jaxpr/ppermute | solution.py:15
  226.8 9.5 %collective-permute-start.1 = (f32[32,512]{1,0:T(8,128)}, f32[32,512]{1,0:T(8,128)}, u32[]{:S(2)}, u32[]{:S(2)}) collective-permute-start(f32[32,512]{1,0:T(8,128)} %fusion.71), channel_id=1, source_target_pairs={{0,32},{32,64},{64,96},{96,128},{128,160},{160,192},{192,224},{224... | collective-permute-start | bytes 196616 | tf_op jit(solution)/shard_map/while/body/eval_jaxpr/ppermute | solution.py:15
  237.2 17.2 %collective-permute-start = (f32[32,512]{1,0:T(8,128)S(1)}, f32[32,512]{1,0:T(8,128)}, u32[]{:S(2)}, u32[]{:S(2)}) collective-permute-start(f32[32,512]{1,0:T(8,128)S(1)} %copy.71), channel_id=1, source_target_pairs={{0,32},{32,64},{64,96},{96,128},{128,160},{160,192},{192,224},{224... | collective-permute-start | bytes 196616 | tf_op jit(solution)/shard_map/while/body/eval_jaxpr/ppermute | solution.py:15
  255.2 17.2 %collective-permute-start = (f32[32,512]{1,0:T(8,128)S(1)}, f32[32,512]{1,0:T(8,128)}, u32[]{:S(2)}, u32[]{:S(2)}) collective-permute-start(f32[32,512]{1,0:T(8,128)S(1)} %copy.71), channel_id=1, source_target_pairs={{0,32},{32,64},{64,96},{96,128},{128,160},{160,192},{192,224},{224... | collective-permute-start | bytes 196616 | tf_op jit(solution)/shard_map/while/body/eval_jaxpr/ppermute | solution.py:15
  262.9 9.5 %collective-permute-start.1 = (f32[32,512]{1,0:T(8,128)}, f32[32,512]{1,0:T(8,128)}, u32[]{:S(2)}, u32[]{:S(2)}) collective-permute-start(f32[32,512]{1,0:T(8,128)} %fusion.71), channel_id=1, source_target_pairs={{0,32},{32,64},{64,96},{96,128},{128,160},{160,192},{192,224},{224... | collective-permute-start | bytes 196616 | tf_op jit(solution)/shard_map/while/body/eval_jaxpr/ppermute | solution.py:15
  273.3 17.2 %collective-permute-start = (f32[32,512]{1,0:T(8,128)S(1)}, f32[32,512]{1,0:T(8,128)}, u32[]{:S(2)}, u32[]{:S(2)}) collective-permute-start(f32[32,512]{1,0:T(8,128)S(1)} %copy.71), channel_id=1, source_target_pairs={{0,32},{32,64},{64,96},{96,128},{128,160},{160,192},{192,224},{224... | collective-permute-start | bytes 196616 | tf_op jit(solution)/shard_map/while/body/eval_jaxpr/ppermute | solution.py:15
  281.0 9.5 %collective-permute-start.1 = (f32[32,512]{1,0:T(8,128)}, f32[32,512]{1,0:T(8,128)}, u32[]{:S(2)}, u32[]{:S(2)}) collective-permute-start(f32[32,512]{1,0:T(8,128)} %fusion.71), channel_id=1, source_target_pairs={{0,32},{32,64},{64,96},{96,128},{128,160},{160,192},{192,224},{224... | collective-permute-start | bytes 196616 | tf_op jit(solution)/shard_map/while/body/eval_jaxpr/ppermute | solution.py:15
  291.3 17.2 %collective-permute-start = (f32[32,512]{1,0:T(8,128)S(1)}, f32[32,512]{1,0:T(8,128)}, u32[]{:S(2)}, u32[]{:S(2)}) collective-permute-start(f32[32,512]{1,0:T(8,128)S(1)} %copy.71), channel_id=1, source_target_pairs={{0,32},{32,64},{64,96},{96,128},{128,160},{160,192},{192,224},{224... | collective-permute-start | bytes 196616 | tf_op jit(solution)/shard_map/while/body/eval_jaxpr/ppermute | solution.py:15
  309.4 17.2 %collective-permute-start = (f32[32,512]{1,0:T(8,128)S(1)}, f32[32,512]{1,0:T(8,128)}, u32[]{:S(2)}, u32[]{:S(2)}) collective-permute-start(f32[32,512]{1,0:T(8,128)S(1)} %copy.71), channel_id=1, source_target_pairs={{0,32},{32,64},{64,96},{96,128},{128,160},{160,192},{192,224},{224... | collective-permute-start | bytes 196616 | tf_op jit(solution)/shard_map/while/body/eval_jaxpr/ppermute | solution.py:15
  317.1 9.5 %collective-permute-start.1 = (f32[32,512]{1,0:T(8,128)}, f32[32,512]{1,0:T(8,128)}, u32[]{:S(2)}, u32[]{:S(2)}) collective-permute-start(f32[32,512]{1,0:T(8,128)} %fusion.71), channel_id=1, source_target_pairs={{0,32},{32,64},{64,96},{96,128},{128,160},{160,192},{192,224},{224... | collective-permute-start | bytes 196616 | tf_op jit(solution)/shard_map/while/body/eval_jaxpr/ppermute | solution.py:15
  327.4 17.2 %collective-permute-start = (f32[32,512]{1,0:T(8,128)S(1)}, f32[32,512]{1,0:T(8,128)}, u32[]{:S(2)}, u32[]{:S(2)}) collective-permute-start(f32[32,512]{1,0:T(8,128)S(1)} %copy.71), channel_id=1, source_target_pairs={{0,32},{32,64},{64,96},{96,128},{128,160},{160,192},{192,224},{224... | collective-permute-start | bytes 196616 | tf_op jit(solution)/shard_map/while/body/eval_jaxpr/ppermute | solution.py:15
  345.5 17.2 %collective-permute-start = (f32[32,512]{1,0:T(8,128)S(1)}, f32[32,512]{1,0:T(8,128)}, u32[]{:S(2)}, u32[]{:S(2)}) collective-permute-start(f32[32,512]{1,0:T(8,128)S(1)} %copy.71), channel_id=1, source_target_pairs={{0,32},{32,64},{64,96},{96,128},{128,160},{160,192},{192,224},{224... | collective-permute-start | bytes 196616 | tf_op jit(solution)/shard_map/while/body/eval_jaxpr/ppermute | solution.py:15
  353.2 9.5 %collective-permute-start.1 = (f32[32,512]{1,0:T(8,128)}, f32[32,512]{1,0:T(8,128)}, u32[]{:S(2)}, u32[]{:S(2)}) collective-permute-start(f32[32,512]{1,0:T(8,128)} %fusion.71), channel_id=1, source_target_pairs={{0,32},{32,64},{64,96},{96,128},{128,160},{160,192},{192,224},{224... | collective-permute-start | bytes 196616 | tf_op jit(solution)/shard_map/while/body/eval_jaxpr/ppermute | solution.py:15
  (11 other events, 81.6 us)
Sparse Core Ops, SparseCore 0:
  362.8 238.8 all-reduce.2
where the time goes:
time: 614 us; the launch traced here: 610 us
  waiting for transfers between devices  236 us (38%)
  starting transfers between devices  117 us (19%)
  matrix products  76 us (12%)
  blocking collectives  69.2 us (11%)
  other arithmetic  65.8 us (11%)
  local copies, waits for them, and re-layouts  30.2 us (5%)
  between operations  14.1 us (2%)
    unnamed x2, waiting for transfers between devices  236 us
    ppermute x32, starting transfers between devices, passed_along(): return lax.ppermute(value, axis, pairs)  117 us
    all_gather x1, blocking collectives, per_device(): caption_group = lax.all_gather(caption_queries, 'wide', axis=0, tiled=True)  69.2 us
    dot_general x48, matrix products, pair_loss(): jnp.einsum('ichp,iphd->ichd', weights, value_heads, precision=lax.Precisi...  44.3 us
    dot_general x48, matrix products, pair_loss(): jnp.einsum('chd,iphd->ichp', query_heads, key_heads, precision=lax.Precis...  31.7 us
    add x16, other arithmetic, cycle_turn(): forward_acc = forward_acc + query_part  24.8 us
    add x16, other arithmetic, cycle_turn(): value_grad + value_part  22.3 us
    while x16, local copies, waits for them, and re-layouts  13.5 us
  transfers between devices with their start and end apart: 33, of which 1 were waited for; matrix products, arithmetic and copies ran while one was open for 25% of the time, Pallas kernels for 0%

commit v1 on v0

--- a/solution.py
+++ b/solution.py
@@ -1,3 +1,4 @@
+import functools
 import jax
 import jax.numpy as jnp
 from jax import lax
@@ -7,6 +8,17 @@
 epsilon = 1e-06
 similarity_multiplier = 10.0
 similarity_shift_term = -2.0
+
+
+def task_fit(my_tile, mesh_ax):
+    res = jnp.stack([my_tile for _ in range(lax.axis_size(mesh_ax))], 0)
+    seen_now = jnp.concatenate(
+        lax.all_to_all(res, axis_name=mesh_ax, split_axis=0, concat_axis=0), 0
+    )
+    return seen_now
+
+
+mix_node_all = functools.partial(task_fit, mesh_ax="wide")
 
 
 def passed_along(value, axis, steps):
@@ -55,7 +67,7 @@
 
 
 def per_device(patch_keys, patch_values, caption_queries, positive):
-    caption_group = lax.all_gather(caption_queries, "wide", axis=0, tiled=True)
+    caption_group = mix_node_all(caption_queries)
     group_rows = caption_group.shape[0]
     cycle_size = lax.axis_size("blk")
     cycle_home = lax.axis_index("blk")

time: 614 us -> 575 us (0.936)
  blocking collectives: 69.2 us -> 0 us
  starting transfers between devices: 117 us -> 133 us
  waiting for transfers between devices: 236 us -> 248 us
    all_gather x1 -> x0, blocking collectives: 69.2 us -> none  [per_device(): caption_group = lax.all_gather(caption_queries, 'wide', axis=0, tiled=True)]
    all_to_all x0 -> x1, starting transfers between devices: none -> 16.5 us  [task_fit(): lax.all_to_all(res, axis_name=mesh_ax, split_axis=0, concat_axis=0)]
    all_to_all x0 -> x1, waiting for transfers between devices: none -> 12.4 us  [task_fit(): lax.all_to_all(res, axis_name=mesh_ax, split_axis=0, concat_axis=0)]
  transfers between devices with their start and end apart: 33 -> 34, of which waited for: 1 -> 2; matrix products, arithmetic and copies ran while one was open for 25% -> 27% of each run, Pallas kernels for 0% -> 0%
where the time goes in v1:
time: 575 us; the launch traced here: 571 us
  waiting for transfers between devices  248 us (43%)
  starting transfers between devices  133 us (23%)
  matrix products  76 us (13%)
  other arithmetic  65.8 us (11%)
  local copies, waits for them, and re-layouts  31.3 us (5%)
  between operations  14.1 us (2%)
    unnamed x2, waiting for transfers between devices  236 us
    ppermute x32, starting transfers between devices, passed_along(): return lax.ppermute(value, axis, pairs)  117 us
    dot_general x48, matrix products, pair_loss(): jnp.einsum('ichp,iphd->ichd', weights, value_heads, precision=lax.Precisi...  44.3 us
    dot_general x48, matrix products, pair_loss(): jnp.einsum('chd,iphd->ichp', query_heads, key_heads, precision=lax.Precis...  31.7 us
    add x16, other arithmetic, cycle_turn(): forward_acc = forward_acc + query_part  24.8 us
    add x16, other arithmetic, cycle_turn(): value_grad + value_part  22.3 us
    all_to_all x1, starting transfers between devices, task_fit(): lax.all_to_all(res, axis_name=mesh_ax, split_axis=0, concat_axis=0)  16.5 us
    while x16, local copies, waits for them, and re-layouts  13.5 us
  transfers between devices with their start and end apart: 34, of which 2 were waited for; matrix products, arithmetic and copies ran while one was open for 27% of the time, Pallas kernels for 0%

profile of v1, /device:TPU:2, one launch (start us, length us, event | category | flops | bytes accessed | tf_op | source)
XLA Modules:
  0.0 571.4 jit_solution(13017560659721302532)
XLA Ops:
  8.5 16.5 %all-to-all-start = ((f32[32,1,512]{2,1,0:T(1,128)}), f32[32,1,512]{2,1,0:T(1,128)S(1)}, u32[]{:S(2)}, u32[]{:S(2)}) async-start(f32[32,1,512]{2,1,0:T(1,128)} %stack.2), calls=%async_computation | async-start | bytes 131072 | tf_op jit(solution)/shard_map/all_to_all | solution.py:16
  26.9 12.4 %all-to-all-done = f32[32,1,512]{2,1,0:T(1,128)S(1)} async-done(((f32[32,1,512]{2,1,0:T(1,128)}), f32[32,1,512]{2,1,0:T(1,128)S(1)}, u32[]{:S(2)}, u32[]{:S(2)}) %all-to-all-start) | async-done | bytes 65568 | tf_op jit(solution)/shard_map/all_to_all | solution.py:16
  40.5 283.0 %while.23 = (s32[]{:T(128)}, f32[1,196,512]{1,2,0:T(8,128)S(1)}, f32[1,196,512]{1,2,0:T(8,128)S(1)}, f32[32,512]{1,0:T(8,128)}, f32[32,512]{1,0:T(8,128)}, /*ind...) while((s32[]{:T(128)}, f32[1,196,512]{1,2,0:T(8,128)S(1)}, ...), condition=%wide.region_7.8_spmd.clone, body=%wide.region_0.7_spmd.clone.sunk | while | flops 232979744 | bytes 9337618 | solution.py:106
  49.0 3.5 collective-permute-start.1
  64.8 3.2 collective-permute-start.1
  80.3 4.8 collective-permute-start.1
  97.5 5.7 %collective-permute-start.1 = (f32[32,512]{1,0:T(8,128)}, f32[32,512]{1,0:T(8,128)}, u32[]{:S(2)}, u32[]{:S(2)}) collective-permute-start(f32[32,512]{1,0:T(8,128)} %fusion.71), channel_id=1, source_target_pairs={{0,32},{32,64},{64,96},{96,128},{128,160},{160,192},{192,224},{224... | collective-permute-start | bytes 196616 | tf_op jit(solution)/shard_map/while/body/eval_jaxpr/ppermute | solution.py:27
  107.8 1.9 collective-permute-start
  115.5 5.7 %collective-permute-start.1 = (f32[32,512]{1,0:T(8,128)}, f32[32,512]{1,0:T(8,128)}, u32[]{:S(2)}, u32[]{:S(2)}) collective-permute-start(f32[32,512]{1,0:T(8,128)} %fusion.71), channel_id=1, source_target_pairs={{0,32},{32,64},{64,96},{96,128},{128,160},{160,192},{192,224},{224... | collective-permute-start | bytes 196616 | tf_op jit(solution)/shard_map/while/body/eval_jaxpr/ppermute | solution.py:27
  133.6 5.7 %collective-permute-start.1 = (f32[32,512]{1,0:T(8,128)}, f32[32,512]{1,0:T(8,128)}, u32[]{:S(2)}, u32[]{:S(2)}) collective-permute-start(f32[32,512]{1,0:T(8,128)} %fusion.71), channel_id=1, source_target_pairs={{0,32},{32,64},{64,96},{96,128},{128,160},{160,192},{192,224},{224... | collective-permute-start | bytes 196616 | tf_op jit(solution)/shard_map/while/body/eval_jaxpr/ppermute | solution.py:27
  143.9 1.9 collective-permute-start
  151.6 5.7 %collective-permute-start.1 = (f32[32,512]{1,0:T(8,128)}, f32[32,512]{1,0:T(8,128)}, u32[]{:S(2)}, u32[]{:S(2)}) collective-permute-start(f32[32,512]{1,0:T(8,128)} %fusion.71), channel_id=1, source_target_pairs={{0,32},{32,64},{64,96},{96,128},{128,160},{160,192},{192,224},{224... | collective-permute-start | bytes 196616 | tf_op jit(solution)/shard_map/while/body/eval_jaxpr/ppermute | solution.py:27
  161.9 1.9 collective-permute-start
  169.6 5.7 %collective-permute-start.1 = (f32[32,512]{1,0:T(8,128)}, f32[32,512]{1,0:T(8,128)}, u32[]{:S(2)}, u32[]{:S(2)}) collective-permute-start(f32[32,512]{1,0:T(8,128)} %fusion.71), channel_id=1, source_target_pairs={{0,32},{32,64},{64,96},{96,128},{128,160},{160,192},{192,224},{224... | collective-permute-start | bytes 196616 | tf_op jit(solution)/shard_map/while/body/eval_jaxpr/ppermute | solution.py:27
  187.7 5.7 %collective-permute-start.1 = (f32[32,512]{1,0:T(8,128)}, f32[32,512]{1,0:T(8,128)}, u32[]{:S(2)}, u32[]{:S(2)}) collective-permute-start(f32[32,512]{1,0:T(8,128)} %fusion.71), channel_id=1, source_target_pairs={{0,32},{32,64},{64,96},{96,128},{128,160},{160,192},{192,224},{224... | collective-permute-start | bytes 196616 | tf_op jit(solution)/shard_map/while/body/eval_jaxpr/ppermute | solution.py:27
  205.7 5.7 %collective-permute-start.1 = (f32[32,512]{1,0:T(8,128)}, f32[32,512]{1,0:T(8,128)}, u32[]{:S(2)}, u32[]{:S(2)}) collective-permute-start(f32[32,512]{1,0:T(8,128)} %fusion.71), channel_id=1, source_target_pairs={{0,32},{32,64},{64,96},{96,128},{128,160},{160,192},{192,224},{224... | collective-permute-start | bytes 196616 | tf_op jit(solution)/shard_map/while/body/eval_jaxpr/ppermute | solution.py:27
  223.8 5.7 %collective-permute-start.1 = (f32[32,512]{1,0:T(8,128)}, f32[32,512]{1,0:T(8,128)}, u32[]{:S(2)}, u32[]{:S(2)}) collective-permute-start(f32[32,512]{1,0:T(8,128)} %fusion.71), channel_id=1, source_target_pairs={{0,32},{32,64},{64,96},{96,128},{128,160},{160,192},{192,224},{224... | collective-permute-start | bytes 196616 | tf_op jit(solution)/shard_map/while/body/eval_jaxpr/ppermute | solution.py:27
  241.8 5.7 %collective-permute-start.1 = (f32[32,512]{1,0:T(8,128)}, f32[32,512]{1,0:T(8,128)}, u32[]{:S(2)}, u32[]{:S(2)}) collective-permute-start(f32[32,512]{1,0:T(8,128)} %fusion.71), channel_id=1, source_target_pairs={{0,32},{32,64},{64,96},{96,128},{128,160},{160,192},{192,224},{224... | collective-permute-start | bytes 196616 | tf_op jit(solution)/shard_map/while/body/eval_jaxpr/ppermute | solution.py:27
  252.2 1.9 collective-permute-start
  259.9 5.7 %collective-permute-start.1 = (f32[32,512]{1,0:T(8,128)}, f32[32,512]{1,0:T(8,128)}, u32[]{:S(2)}, u32[]{:S(2)}) collective-permute-start(f32[32,512]{1,0:T(8,128)} %fusion.71), channel_id=1, source_target_pairs={{0,32},{32,64},{64,96},{96,128},{128,160},{160,192},{192,224},{224... | collective-permute-start | bytes 196616 | tf_op jit(solution)/shard_map/while/body/eval_jaxpr/ppermute | solution.py:27
  277.9 5.7 %collective-permute-start.1 = (f32[32,512]{1,0:T(8,128)}, f32[32,512]{1,0:T(8,128)}, u32[]{:S(2)}, u32[]{:S(2)}) collective-permute-start(f32[32,512]{1,0:T(8,128)} %fusion.71), channel_id=1, source_target_pairs={{0,32},{32,64},{64,96},{96,128},{128,160},{160,192},{192,224},{224... | collective-permute-start | bytes 196616 | tf_op jit(solution)/shard_map/while/body/eval_jaxpr/ppermute | solution.py:27
  296.0 5.7 %collective-permute-start.1 = (f32[32,512]{1,0:T(8,128)}, f32[32,512]{1,0:T(8,128)}, u32[]{:S(2)}, u32[]{:S(2)}) collective-permute-start(f32[32,512]{1,0:T(8,128)} %fusion.71), channel_id=1, source_target_pairs={{0,32},{32,64},{64,96},{96,128},{128,160},{160,192},{192,224},{224... | collective-permute-start | bytes 196616 | tf_op jit(solution)/shard_map/while/body/eval_jaxpr/ppermute | solution.py:27
  314.0 5.7 %collective-permute-start.1 = (f32[32,512]{1,0:T(8,128)}, f32[32,512]{1,0:T(8,128)}, u32[]{:S(2)}, u32[]{:S(2)}) collective-permute-start(f32[32,512]{1,0:T(8,128)} %fusion.71), channel_id=1, source_target_pairs={{0,32},{32,64},{64,96},{96,128},{128,160},{160,192},{192,224},{224... | collective-permute-start | bytes 196616 | tf_op jit(solution)/shard_map/while/body/eval_jaxpr/ppermute | solution.py:27
  326.8 235.9 %all-reduce.3.cloned.1.call-done = f32[32,512]{1,0:T(8,128)} async-done(((f32[32,512]{1,0:T(8,128)}), f32[32,512]{1,0:T(8,128)}) %all-reduce.3.cloned.1.call-update) | async-done | bytes 65552
  (411 shorter events, 196.2 us)
Async XLA Ops:
  8.5 30.7 %all-to-all-start = ((f32[32,1,512]{2,1,0:T(1,128)}), f32[32,1,512]{2,1,0:T(1,128)S(1)}, u32[]{:S(2)}, u32[]{:S(2)}) async-start(f32[32,1,512]{2,1,0:T(1,128)} %stack.2), calls=%async_computation | async-start | bytes 131072 | tf_op jit(solution)/shard_map/all_to_all | solution.py:16
  25.0 537.7 %all-reduce.3.cloned.1.call-start = ((), (), s32[]{:S(2)}) async-start(), calls=%async_computation.1 | async-start | bytes 131072
  41.3 14.9 %collective-permute-start = (f32[32,512]{1,0:T(8,128)S(1)}, f32[32,512]{1,0:T(8,128)}, u32[]{:S(2)}, u32[]{:S(2)}) collective-permute-start(f32[32,512]{1,0:T(8,128)S(1)} %copy.71), channel_id=1, source_target_pairs={{0,32},{32,64},{64,96},{96,128},{128,160},{160,192},{192,224},{224... | collective-permute-start | bytes 196616 | tf_op jit(solution)/shard_map/while/body/eval_jaxpr/ppermute | solution.py:27
  57.1 14.6 %collective-permute-start = (f32[32,512]{1,0:T(8,128)S(1)}, f32[32,512]{1,0:T(8,128)}, u32[]{:S(2)}, u32[]{:S(2)}) collective-permute-start(f32[32,512]{1,0:T(8,128)S(1)} %copy.71), channel_id=1, source_target_pairs={{0,32},{32,64},{64,96},{96,128},{128,160},{160,192},{192,224},{224... | collective-permute-start | bytes 196616 | tf_op jit(solution)/shard_map/while/body/eval_jaxpr/ppermute | solution.py:27
  72.6 16.3 %collective-permute-start = (f32[32,512]{1,0:T(8,128)S(1)}, f32[32,512]{1,0:T(8,128)}, u32[]{:S(2)}, u32[]{:S(2)}) collective-permute-start(f32[32,512]{1,0:T(8,128)S(1)} %copy.71), channel_id=1, source_target_pairs={{0,32},{32,64},{64,96},{96,128},{128,160},{160,192},{192,224},{224... | collective-permute-start | bytes 196616 | tf_op jit(solution)/shard_map/while/body/eval_jaxpr/ppermute | solution.py:27
  89.8 17.2 %collective-permute-start = (f32[32,512]{1,0:T(8,128)S(1)}, f32[32,512]{1,0:T(8,128)}, u32[]{:S(2)}, u32[]{:S(2)}) collective-permute-start(f32[32,512]{1,0:T(8,128)S(1)} %copy.71), channel_id=1, source_target_pairs={{0,32},{32,64},{64,96},{96,128},{128,160},{160,192},{192,224},{224... | collective-permute-start | bytes 196616 | tf_op jit(solution)/shard_map/while/body/eval_jaxpr/ppermute | solution.py:27
  107.8 17.2 %collective-permute-start = (f32[32,512]{1,0:T(8,128)S(1)}, f32[32,512]{1,0:T(8,128)}, u32[]{:S(2)}, u32[]{:S(2)}) collective-permute-start(f32[32,512]{1,0:T(8,128)S(1)} %copy.71), channel_id=1, source_target_pairs={{0,32},{32,64},{64,96},{96,128},{128,160},{160,192},{192,224},{224... | collective-permute-start | bytes 196616 | tf_op jit(solution)/shard_map/while/body/eval_jaxpr/ppermute | solution.py:27
  125.9 17.2 %collective-permute-start = (f32[32,512]{1,0:T(8,128)S(1)}, f32[32,512]{1,0:T(8,128)}, u32[]{:S(2)}, u32[]{:S(2)}) collective-permute-start(f32[32,512]{1,0:T(8,128)S(1)} %copy.71), channel_id=1, source_target_pairs={{0,32},{32,64},{64,96},{96,128},{128,160},{160,192},{192,224},{224... | collective-permute-start | bytes 196616 | tf_op jit(solution)/shard_map/while/body/eval_jaxpr/ppermute | solution.py:27
  133.6 9.5 %collective-permute-start.1 = (f32[32,512]{1,0:T(8,128)}, f32[32,512]{1,0:T(8,128)}, u32[]{:S(2)}, u32[]{:S(2)}) collective-permute-start(f32[32,512]{1,0:T(8,128)} %fusion.71), channel_id=1, source_target_pairs={{0,32},{32,64},{64,96},{96,128},{128,160},{160,192},{192,224},{224... | collective-permute-start | bytes 196616 | tf_op jit(solution)/shard_map/while/body/eval_jaxpr/ppermute | solution.py:27
  143.9 17.2 %collective-permute-start = (f32[32,512]{1,0:T(8,128)S(1)}, f32[32,512]{1,0:T(8,128)}, u32[]{:S(2)}, u32[]{:S(2)}) collective-permute-start(f32[32,512]{1,0:T(8,128)S(1)} %copy.71), channel_id=1, source_target_pairs={{0,32},{32,64},{64,96},{96,128},{128,160},{160,192},{192,224},{224... | collective-permute-start | bytes 196616 | tf_op jit(solution)/shard_map/while/body/eval_jaxpr/ppermute | solution.py:27
  161.9 17.2 %collective-permute-start = (f32[32,512]{1,0:T(8,128)S(1)}, f32[32,512]{1,0:T(8,128)}, u32[]{:S(2)}, u32[]{:S(2)}) collective-permute-start(f32[32,512]{1,0:T(8,128)S(1)} %copy.71), channel_id=1, source_target_pairs={{0,32},{32,64},{64,96},{96,128},{128,160},{160,192},{192,224},{224... | collective-permute-start | bytes 196616 | tf_op jit(solution)/shard_map/while/body/eval_jaxpr/ppermute | solution.py:27
  169.6 9.5 %collective-permute-start.1 = (f32[32,512]{1,0:T(8,128)}, f32[32,512]{1,0:T(8,128)}, u32[]{:S(2)}, u32[]{:S(2)}) collective-permute-start(f32[32,512]{1,0:T(8,128)} %fusion.71), channel_id=1, source_target_pairs={{0,32},{32,64},{64,96},{96,128},{128,160},{160,192},{192,224},{224... | collective-permute-start | bytes 196616 | tf_op jit(solution)/shard_map/while/body/eval_jaxpr/ppermute | solution.py:27
  180.0 17.2 %collective-permute-start = (f32[32,512]{1,0:T(8,128)S(1)}, f32[32,512]{1,0:T(8,128)}, u32[]{:S(2)}, u32[]{:S(2)}) collective-permute-start(f32[32,512]{1,0:T(8,128)S(1)} %copy.71), channel_id=1, source_target_pairs={{0,32},{32,64},{64,96},{96,128},{128,160},{160,192},{192,224},{224... | collective-permute-start | bytes 196616 | tf_op jit(solution)/shard_map/while/body/eval_jaxpr/ppermute | solution.py:27
  198.0 17.2 %collective-permute-start = (f32[32,512]{1,0:T(8,128)S(1)}, f32[32,512]{1,0:T(8,128)}, u32[]{:S(2)}, u32[]{:S(2)}) collective-permute-start(f32[32,512]{1,0:T(8,128)S(1)} %copy.71), channel_id=1, source_target_pairs={{0,32},{32,64},{64,96},{96,128},{128,160},{160,192},{192,224},{224... | collective-permute-start | bytes 196616 | tf_op jit(solution)/shard_map/while/body/eval_jaxpr/ppermute | solution.py:27
  205.7 9.5 %collective-permute-start.1 = (f32[32,512]{1,0:T(8,128)}, f32[32,512]{1,0:T(8,128)}, u32[]{:S(2)}, u32[]{:S(2)}) collective-permute-start(f32[32,512]{1,0:T(8,128)} %fusion.71), channel_id=1, source_target_pairs={{0,32},{32,64},{64,96},{96,128},{128,160},{160,192},{192,224},{224... | collective-permute-start | bytes 196616 | tf_op jit(solution)/shard_map/while/body/eval_jaxpr/ppermute | solution.py:27
  216.1 17.2 %collective-permute-start = (f32[32,512]{1,0:T(8,128)S(1)}, f32[32,512]{1,0:T(8,128)}, u32[]{:S(2)}, u32[]{:S(2)}) collective-permute-start(f32[32,512]{1,0:T(8,128)S(1)} %copy.71), channel_id=1, source_target_pairs={{0,32},{32,64},{64,96},{96,128},{128,160},{160,192},{192,224},{224... | collective-permute-start | bytes 196616 | tf_op jit(solution)/shard_map/while/body/eval_jaxpr/ppermute | solution.py:27
  223.8 9.5 %collective-permute-start.1 = (f32[32,512]{1,0:T(8,128)}, f32[32,512]{1,0:T(8,128)}, u32[]{:S(2)}, u32[]{:S(2)}) collective-permute-start(f32[32,512]{1,0:T(8,128)} %fusion.71), channel_id=1, source_target_pairs={{0,32},{32,64},{64,96},{96,128},{128,160},{160,192},{192,224},{224... | collective-permute-start | bytes 196616 | tf_op jit(solution)/shard_map/while/body/eval_jaxpr/ppermute | solution.py:27
  234.1 17.2 %collective-permute-start = (f32[32,512]{1,0:T(8,128)S(1)}, f32[32,512]{1,0:T(8,128)}, u32[]{:S(2)}, u32[]{:S(2)}) collective-permute-start(f32[32,512]{1,0:T(8,128)S(1)} %copy.71), channel_id=1, source_target_pairs={{0,32},{32,64},{64,96},{96,128},{128,160},{160,192},{192,224},{224... | collective-permute-start | bytes 196616 | tf_op jit(solution)/shard_map/while/body/eval_jaxpr/ppermute | solution.py:27
  252.2 17.2 %collective-permute-start = (f32[32,512]{1,0:T(8,128)S(1)}, f32[32,512]{1,0:T(8,128)}, u32[]{:S(2)}, u32[]{:S(2)}) collective-permute-start(f32[32,512]{1,0:T(8,128)S(1)} %copy.71), channel_id=1, source_target_pairs={{0,32},{32,64},{64,96},{96,128},{128,160},{160,192},{192,224},{224... | collective-permute-start | bytes 196616 | tf_op jit(solution)/shard_map/while/body/eval_jaxpr/ppermute | solution.py:27
  259.9 9.5 %collective-permute-start.1 = (f32[32,512]{1,0:T(8,128)}, f32[32,512]{1,0:T(8,128)}, u32[]{:S(2)}, u32[]{:S(2)}) collective-permute-start(f32[32,512]{1,0:T(8,128)} %fusion.71), channel_id=1, source_target_pairs={{0,32},{32,64},{64,96},{96,128},{128,160},{160,192},{192,224},{224... | collective-permute-start | bytes 196616 | tf_op jit(solution)/shard_map/while/body/eval_jaxpr/ppermute | solution.py:27
  270.2 17.2 %collective-permute-start = (f32[32,512]{1,0:T(8,128)S(1)}, f32[32,512]{1,0:T(8,128)}, u32[]{:S(2)}, u32[]{:S(2)}) collective-permute-start(f32[32,512]{1,0:T(8,128)S(1)} %copy.71), channel_id=1, source_target_pairs={{0,32},{32,64},{64,96},{96,128},{128,160},{160,192},{192,224},{224... | collective-permute-start | bytes 196616 | tf_op jit(solution)/shard_map/while/body/eval_jaxpr/ppermute | solution.py:27
  288.3 17.2 %collective-permute-start = (f32[32,512]{1,0:T(8,128)S(1)}, f32[32,512]{1,0:T(8,128)}, u32[]{:S(2)}, u32[]{:S(2)}) collective-permute-start(f32[32,512]{1,0:T(8,128)S(1)} %copy.71), channel_id=1, source_target_pairs={{0,32},{32,64},{64,96},{96,128},{128,160},{160,192},{192,224},{224... | collective-permute-start | bytes 196616 | tf_op jit(solution)/shard_map/while/body/eval_jaxpr/ppermute | solution.py:27
  296.0 9.5 %collective-permute-start.1 = (f32[32,512]{1,0:T(8,128)}, f32[32,512]{1,0:T(8,128)}, u32[]{:S(2)}, u32[]{:S(2)}) collective-permute-start(f32[32,512]{1,0:T(8,128)} %fusion.71), channel_id=1, source_target_pairs={{0,32},{32,64},{64,96},{96,128},{128,160},{160,192},{192,224},{224... | collective-permute-start | bytes 196616 | tf_op jit(solution)/shard_map/while/body/eval_jaxpr/ppermute | solution.py:27
  306.3 17.2 %collective-permute-start = (f32[32,512]{1,0:T(8,128)S(1)}, f32[32,512]{1,0:T(8,128)}, u32[]{:S(2)}, u32[]{:S(2)}) collective-permute-start(f32[32,512]{1,0:T(8,128)S(1)} %copy.71), channel_id=1, source_target_pairs={{0,32},{32,64},{64,96},{96,128},{128,160},{160,192},{192,224},{224... | collective-permute-start | bytes 196616 | tf_op jit(solution)/shard_map/while/body/eval_jaxpr/ppermute | solution.py:27
  (11 other events, 90.4 us)
Sparse Core Ops, SparseCore 0:
  323.6 238.9 all-reduce.2
